TPU v7x, 256 devices: a whole 4x4x8 slice. The times are simulated.
256 devices in a mesh: lon: 32 (over z, y_hi, core), lat: 8 (over y_lo, x).
Axes of the slice: x: 4, y: 4 (y_hi: 2, y_lo: 2; y = y_hi * 2 + y_lo), z: 8, core: 2. Of those that a mesh axis runs over, the one named last changes fastest.
Arguments:
- state: bfloat16 [360, 768, 128], P('lat', 'lon'), may hold values from -6 to 6
- land_sea: int32 [360, 768], P('lat', 'lon'), may hold values 0 or 1
- cotangent: bfloat16 [360, 768, 128], P('lat', 'lon'), may hold values from -6 to 6
- dw_kernel: bfloat16 [2, 7, 7, 128], replicated, may hold values from -0.875 to 0.875
- conv_bias: float32 [2, 128], replicated, may hold values from -3 to 3
- norm_gain: float32 [2, 128], replicated, may hold values from 0.1 to 1.9
- norm_bias: float32 [2, 128], replicated, may hold values from -3 to 3
- weight_in: bfloat16 [2, 128, 512], replicated, may hold values from -0.5 to 0.5
- bias_in: float32 [2, 512], replicated, may hold values from -3 to 3
- weight_out: bfloat16 [2, 512, 128], replicated, may hold values from -0.25 to 0.25
- bias_out: float32 [2, 128], replicated, may hold values from -3 to 3
- layer_scale: float32 [2, 128], replicated, may hold values from 0.3 to 1
Outputs:
- output: bfloat16 [360, 768, 128], P('lat', 'lon')
- grad_state: bfloat16 [360, 768, 128], P('lat', 'lon')
- grad_dw_kernel: float32 [2, 7, 7, 128], replicated
- grad_conv_bias: float32 [2, 128], replicated
- grad_norm_gain: float32 [2, 128], replicated
- grad_norm_bias: float32 [2, 128], replicated
- grad_weight_in: float32 [2, 128, 512], replicated
- grad_bias_in: float32 [2, 512], replicated
- grad_weight_out: float32 [2, 512, 128], replicated
- grad_bias_out: float32 [2, 128], replicated
- grad_layer_scale: float32 [2, 128], replicated
All inputs are finite; a program needn't handle non-finite values. No bound on the sum of `land_sea` on one device may be relied on, other than what follows from the above.
Results may differ from a plain program's by a relative error of at most 0.02.
Values may be sent and summed in bfloat16 or wider, within the bound.
A program may use at most 64 MiB of HBM per device.

v0:
```python
import math
import jax
import jax.numpy as jnp
from jax import lax
from jax.sharding import PartitionSpec as P

KSIZE = 7
BLOCKS = 2
EPS_NORM = 1e-06
INV_ROOT_TWO = 0.7071067811865476
INV_ROOT_TWO_PI = 0.3989422804014327


def with_halo(shard, sides, width, wrap):
    for axis, dim in sides:
        count, length = (lax.axis_size(axis), shard.shape[dim])
        up = [(i, (i + 1) % count) for i in range(count if wrap else count - 1)]
        down = [(j, i) for i, j in up]
        last = lax.slice_in_dim(shard, length - width, length, axis=dim)
        first = lax.slice_in_dim(shard, 0, width, axis=dim)
        before = lax.ppermute(last, axis, up)
        after = lax.ppermute(first, axis, down)
        shard = jnp.concatenate([before, shard, after], axis=dim)
    return shard


def depthwise(window, kernel, height, breadth):
    summed = jnp.zeros((height, breadth, window.shape[2]), jnp.float32)
    for tap_row in range(KSIZE):
        for tap_col in range(KSIZE):
            piece = window[tap_row : tap_row + height, tap_col : tap_col + breadth].astype(
                jnp.float32
            )
            summed = summed + piece * kernel[tap_row, tap_col].astype(jnp.float32)
    return summed


def block_forward(window, land_rows, params):
    (
        kernel,
        conv_bias,
        norm_gain,
        norm_bias,
        weight_in,
        bias_in,
        weight_out,
        bias_out,
        layer_scale,
    ) = params
    margin = KSIZE // 2
    height = window.shape[0] - 2 * margin
    breadth = window.shape[1] - 2 * margin
    channels = window.shape[2]
    cell_count = height * breadth
    mixed_sum = depthwise(window, kernel, height, breadth) + conv_bias
    center = mixed_sum - jnp.mean(mixed_sum, axis=-1, keepdims=True)
    inverse = lax.rsqrt(jnp.mean(center * center, axis=-1, keepdims=True) + EPS_NORM)
    normed = (center * inverse).reshape(cell_count, channels)
    lifted = (normed * norm_gain + norm_bias).astype(jnp.bfloat16)
    hidden = jnp.dot(lifted, weight_in, preferred_element_type=jnp.float32) + bias_in
    active = jax.nn.gelu(hidden, approximate=False).astype(jnp.bfloat16)
    branch = jnp.dot(active, weight_out, preferred_element_type=jnp.float32) + bias_out
    interior = (
        window[margin : margin + height, margin : margin + breadth]
        .astype(jnp.float32)
        .reshape(cell_count, channels)
    )
    ocean_mask = land_rows.reshape(cell_count, 1).astype(jnp.float32)
    result = (
        ((interior + layer_scale * branch) * ocean_mask)
        .astype(jnp.bfloat16)
        .reshape(height, breadth, channels)
    )
    return (result, (normed, inverse.reshape(cell_count, 1), lifted, hidden, active, branch))


def block_backward(window, land_rows, incoming, params, stored):
    (
        kernel,
        conv_bias,
        norm_gain,
        norm_bias,
        weight_in,
        bias_in,
        weight_out,
        bias_out,
        layer_scale,
    ) = params
    normed, inverse, lifted, hidden, active, branch = stored
    margin = KSIZE // 2
    height = window.shape[0] - 2 * margin
    breadth = window.shape[1] - 2 * margin
    channels = window.shape[2]
    cell_count = height * breadth
    ocean_mask = land_rows.reshape(cell_count, 1).astype(jnp.float32)
    masked = incoming.reshape(cell_count, channels).astype(jnp.float32) * ocean_mask
    grad_branch = (masked * layer_scale).astype(jnp.bfloat16)
    contract_rows = (((0,), (0,)), ((), ()))
    contract_cols = (((1,), (1,)), ((), ()))
    grad_scale = jnp.sum(masked * branch, axis=0)
    grad_bias_out = jnp.sum(grad_branch.astype(jnp.float32), axis=0)
    grad_weight_out = lax.dot_general(
        active, grad_branch, contract_rows, preferred_element_type=jnp.float32
    )
    grad_active = lax.dot_general(
        grad_branch, weight_out, contract_cols, preferred_element_type=jnp.float32
    )
    cumulative = 0.5 * (1.0 + lax.erf(hidden * INV_ROOT_TWO))
    density = jnp.exp(-0.5 * hidden * hidden) * INV_ROOT_TWO_PI
    grad_hidden = (grad_active * (cumulative + hidden * density)).astype(jnp.bfloat16)
    grad_bias_in = jnp.sum(grad_hidden.astype(jnp.float32), axis=0)
    grad_weight_in = lax.dot_general(
        lifted, grad_hidden, contract_rows, preferred_element_type=jnp.float32
    )
    grad_lifted = lax.dot_general(
        grad_hidden, weight_in, contract_cols, preferred_element_type=jnp.float32
    )
    grad_gain = jnp.sum(grad_lifted * normed, axis=0)
    grad_shift = jnp.sum(grad_lifted, axis=0)
    scaled = grad_lifted * norm_gain
    grad_mixed = inverse * (
        scaled
        - jnp.mean(scaled, axis=-1, keepdims=True)
        - normed * jnp.mean(scaled * normed, axis=-1, keepdims=True)
    )
    grad_mixed = grad_mixed.astype(jnp.bfloat16).reshape(height, breadth, channels)
    spread = grad_mixed.astype(jnp.float32)
    grad_conv_bias = jnp.sum(spread, axis=(0, 1))
    tap_sums = []
    for tap_row in range(KSIZE):
        for tap_col in range(KSIZE):
            piece = window[tap_row : tap_row + height, tap_col : tap_col + breadth].astype(
                jnp.float32
            )
            tap_sums.append(jnp.sum(spread * piece, axis=(0, 1)))
    grad_kernel = jnp.stack(tap_sums).reshape(KSIZE, KSIZE, channels)
    gradients = (
        grad_kernel,
        grad_conv_bias,
        grad_gain,
        grad_shift,
        grad_weight_in,
        grad_bias_in,
        grad_weight_out,
        grad_bias_out,
        grad_scale,
    )
    return (grad_mixed, masked.reshape(height, breadth, channels), gradients)


def adjoint(padded, masked, kernel):
    margin = KSIZE // 2
    height = masked.shape[0]
    breadth = masked.shape[1]
    summed = masked
    for tap_row in range(KSIZE):
        for tap_col in range(KSIZE):
            first_row = 2 * margin - tap_row
            first_col = 2 * margin - tap_col
            piece = padded[first_row : first_row + height, first_col : first_col + breadth].astype(
                jnp.float32
            )
            summed = summed + piece * kernel[tap_row, tap_col].astype(jnp.float32)
    return summed.astype(jnp.bfloat16)


def extend(tile_field):
    beside_all = with_halo(tile_field, (("lon", 1),), KSIZE // 2, True)
    return with_halo(beside_all, (("lat", 0),), KSIZE // 2, False)


def sum_everything(parts):
    (
        kernel_part,
        conv_part,
        gain_part,
        shift_part,
        first_part,
        first_bias,
        second_part,
        second_bias,
        scale_part,
    ) = parts
    return lax.psum(
        (
            kernel_part,
            conv_part,
            gain_part,
            shift_part,
            first_part,
            first_bias,
            second_part,
            second_bias,
            scale_part,
        ),
        ("lon", "lat"),
    )


def on_device(
    state,
    land_sea,
    cotangent,
    dw_kernel,
    conv_bias,
    norm_gain,
    norm_bias,
    weight_in,
    bias_in,
    weight_out,
    bias_out,
    layer_scale,
):
    stacked = (
        dw_kernel,
        conv_bias,
        norm_gain,
        norm_bias,
        weight_in,
        bias_in,
        weight_out,
        bias_out,
        layer_scale,
    )
    height = state.shape[0]
    breadth = state.shape[1]
    grad_norm = 1.0 / math.sqrt(lax.axis_size("lat") * height * lax.axis_size("lon") * breadth)
    current = state
    windows = []
    stored_all = []
    for layer_index in range(BLOCKS):
        params = tuple((member[layer_index] for member in stacked))
        window = extend(current)
        windows.append(window)
        outcome = block_forward(window, land_sea, params)
        current = outcome[0]
        stored_all.append(outcome[1])
    incoming = cotangent
    per_layer = [None] * BLOCKS
    for layer_index in reversed(range(BLOCKS)):
        params = tuple((member[layer_index] for member in stacked))
        stored = stored_all[layer_index]
        grad_mixed, masked, gradients = block_backward(
            windows[layer_index], land_sea, incoming, params, stored
        )
        incoming = adjoint(extend(grad_mixed), masked, params[0])
        per_layer[layer_index] = gradients
    combined = tuple(
        (
            jnp.stack([per_layer[layer_index][member] for layer_index in range(BLOCKS)])
            for member in range(9)
        )
    )
    combined = sum_everything(combined)
    scaled = [member * grad_norm for member in combined]
    return (
        current,
        incoming,
        scaled[0],
        scaled[1],
        scaled[2],
        scaled[3],
        scaled[4],
        scaled[5],
        scaled[6],
        scaled[7],
        scaled[8],
    )


def solution(mesh):
    placed = (
        P("lat", "lon", None),
        P("lat", "lon"),
        P("lat", "lon", None),
        P(),
        P(),
        P(),
        P(),
        P(),
        P(),
        P(),
        P(),
        P(),
    )
    return jax.shard_map(
        on_device,
        mesh=mesh,
        in_specs=placed,
        out_specs=(
            P("lat", "lon", None),
            P("lat", "lon", None),
            P(),
            P(),
            P(),
            P(),
            P(),
            P(),
            P(),
            P(),
            P(),
        ),
        check_vma=False,
    )
```

profile of v0, /device:TPU:2, one launch (start us, length us, event | category | flops | bytes accessed | tf_op | source)
XLA Modules:
  0.0 509.7 jit_solution(3118116453118885206)
XLA Ops:
  8.3 8.0 %collective-permute-start.1 = (bf16[45,3,128]{2,1,0:T(4,128)(2,1)S(1)}, bf16[45,3,128]{2,1,0:T(4,128)(2,1)S(1)}, u32[]{:S(2)}, u32[]{:S(2)}) collective-permute-start(bf16[45,3,128]{2,1,0:T(4,128)(2,1)S(1)} %get-tuple-element.208), channel_id=1, source_target_pairs={{8,0},{16,8},{24,16},{32,24},{40,32},{48,40},{56,48},{64,56},{72,6... | collective-permute-start | bytes 103688 | tf_op jit(solution)/shard_map/ppermute | solution.py:22
  24.9 2.5 convert_reduce_fusion.3
  29.2 3.4 collective-permute-start.2
  32.6 2.4 collective-permute-start.3
  35.1 3.2 collective-permute-done.3
  38.6 5.0 fusion.421
  44.7 6.0 %fusion.4 = (bf16[1080,512]{1,0:T(8,128)(2,1)S(1)}, f32[1080,512]{1,0:T(8,128)}) fusion(f32[512]{0:T(512)S(1)} %bitcast.782, bf16[1080,128]{1,0:T(8,128)(2,1)S(1)} %bitcast.742, bf16[2,128,512]{2,1,0:T(8,128)(2,1)S(1)} %copy-done.11), kind=kOutput, calls=%fused_computation.113 | convolution fusion | flops 178053120 | bytes 3727360 | tf_op jit(solution)/shard_map/dot_general | solution.py:60
  53.2 5.3 %collective-permute-start.5 = (bf16[45,3,128]{2,1,0:T(4,128)(2,1)S(1)}, bf16[45,3,128]{2,1,0:T(4,128)(2,1)S(1)}, u32[]{:S(2)}, u32[]{:S(2)}) collective-permute-start(bf16[45,3,128]{2,1,0:T(4,128)(2,1)S(1)} %get-tuple-element.206), channel_id=1, source_target_pairs={{8,0},{16,8},{24,16},{32,24},{40,32},{48,40},{56,48},{64,56},{72,6... | collective-permute-start | bytes 103688 | tf_op jit(solution)/shard_map/ppermute | solution.py:22
  60.3 3.1 collective-permute-start.6
  63.4 3.1 collective-permute-start.7
  66.8 3.1 collective-permute-done.7
  70.1 5.0 fusion.419
  78.7 7.0 %fusion.7 = (bf16[1080,512]{1,0:T(8,128)(2,1)}, f32[1080,512]{1,0:T(8,128)S(1)}) fusion(f32[512]{0:T(512)} %bitcast.780, bf16[1080,128]{1,0:T(8,128)(2,1)S(1)} %bitcast.741, bf16[2,128,512]{2,1,0:T(8,128)(2,1)} %param.19), kind=kOutput, calls=%fused_computation.116 | convolution fusion | flops 178053120 | bytes 3727360 | tf_op jit(solution)/shard_map/dot_general | solution.py:60
  85.7 1.9 convert_reduce_fusion
  93.1 5.3 %collective-permute-start.9 = (bf16[45,3,128]{2,1,0:T(4,128)(2,1)S(1)}, bf16[45,3,128]{2,1,0:T(4,128)(2,1)S(1)}, u32[]{:S(2)}, u32[]{:S(2)}) collective-permute-start(bf16[45,3,128]{2,1,0:T(4,128)(2,1)S(1)} %get-tuple-element.204), channel_id=1, source_target_pairs={{8,0},{16,8},{24,16},{32,24},{40,32},{48,40},{56,48},{64,56},{72,6... | collective-permute-start | bytes 103688 | tf_op jit(solution)/shard_map/ppermute | solution.py:22
  98.4 1.7 fusion.200
  100.4 2.2 collective-permute-start.10
  102.6 12.7 %collective-permute-start.11 = (bf16[3,30,128]{2,1,0:T(8,128)(2,1)S(1)}, bf16[3,30,128]{2,1,0:T(8,128)(2,1)S(1)}, u32[]{:S(2)}, u32[]{:S(2)}) collective-permute-start(bf16[3,30,128]{2,1,0:T(8,128)(2,1)S(1)} %get-tuple-element.191), channel_id=1, source_target_pairs={{0,1},{1,2},{2,3},{3,4},{4,5},{5,6},{6,7},{8,9},{9,10},{10,11},{11... | collective-permute-start | bytes 69128 | tf_op jit(solution)/shard_map/ppermute | solution.py:21
  115.8 4.9 stack.474
  122.0 6.2 %multiply_convert_fusion.1 = (bf16[1080,128]{1,0:T(8,128)(2,1)S(1)}, bf16[45,24,128]{2,1,0:T(8,128)(2,1)S(1)}) fusion(f32[1080]{0:T(1024)S(1)} %convert_element_type.1163, f32[128]{0:T(128)S(1)} %copy-done.21, f32[128]{0:T(128)S(1)} %copy-done.102, bf16[48,30,128]{2,1,0:T(8,128)(2,1)S(1)} %get-tuple-element.189, f32[128]{0:T(128)S(1)} %copy-done.104, ...), kind=kLoop, calls=%fused_computation.516 | loop fusion | flops 23777280 | bytes 12821440 | tf_op jit(solution)/shard_map/convert_element_type | solution.py:97
  128.5 1.9 convert_reduce_fusion.1
  133.0 1.6 fusion.247
  134.6 1.6 fusion.275
  137.5 2.4 multiply_reduce_fusion.1
  143.8 81.3 %all-reduce = (f32[2,7,7,128]{3,2,1,0:T(8,128)S(1)}, f32[2,128]{1,0:T(2,128)S(1)}, f32[2,128]{1,0:T(2,128)S(1)}, f32[2,128]{1,0:T(2,128)S(1)}, f32[2,512]{1,0:T(...) all-reduce(f32[2,7,7,128]{3,2,1,0:T(8,128)S(1)} %pad_maximum_fusion, ...), channel_id=1, replica_groups=mesh['lon'=32,'lat'=8] {'lon','lat'}, use_global_device_ids=true, to_apply=%region_106.0 | all-reduce | flops 14848 | bytes 118784 | tf_op jit(solution)/shard_map/psum | solution.py:184
  230.7 6.0 %collective-permute-done.12 = bf16[45,3,128]{2,1,0:T(4,128)(2,1)S(1)} collective-permute-done((bf16[45,3,128]{2,1,0:T(4,128)(2,1)S(1)}, bf16[45,3,128]{2,1,0:T(4,128)(2,1)S(1)}, u32[]{:S(2)}, u32[]{:S(2)}) %collective-permute-start.12) | collective-permute-done | bytes 34592 | tf_op jit(solution)/shard_map/ppermute | solution.py:21
  236.7 2.6 collective-permute-start.14
  239.3 3.2 collective-permute-start.15
  245.6 5.8 %fusion.280 = bf16[45,24,128]{2,1,0:T(8,128)(2,1)} fusion(bf16[45,24,128]{2,1,0:T(8,128)(2,1)S(1)} %bitcast.724, bf16[45,24,128]{2,1,0:T(8,128)(2,1)S(1)} %get-tuple-element.167, bf16[45,3,128]{2,1,0:T(4,128)(2,1)S(1)} %collective-permute-done.12, bf16[45,3,128]{2,1,0:T(4,128)(2,1)S(1)} %collective-permute-done.13, ...), kind=kLoop, calls=%fused_computation.534 | loop fusion | flops 23224320 | bytes 12540128 | tf_op jit(solution)/shard_map/convert_element_type | solution.py:164
  251.4 247.4 %all-reduce.4.cloned.1.call-done = (f32[2,128,512]{2,1,0:T(8,128)}, f32[2,512,128]{2,1,0:T(8,128)}) async-done(((f32[2,128,512]{2,1,0:T(8,128)}, f32[2,512,128]{2,1,0:T(8,128)}), (f32[2,128,512]{2,1,0:T(8,128)}, f32[2,512,128]{2,1,0:T(8,128)})) %all-reduce.4.cloned.1.call-update) | async-done | bytes 1048592 | tf_op jit(solution)/shard_map/psum | solution.py:184
  498.8 1.9 broadcast_multiply_fusion.1
  500.7 1.9 broadcast_multiply_fusion
  (468 shorter events, 42.6 us)
Async XLA Ops:
  7.2 31.2 %copy-start = (bf16[45,24,128]{2,1,0:T(8,128)(2,1)S(1)}, bf16[45,24,128]{2,1,0:T(8,128)(2,1)}, u32[]{:S(2)}) copy-start(bf16[45,24,128]{2,1,0:T(8,128)(2,1)} %param.12) | copy-start | bytes 829444
  7.2 491.6 %all-reduce.4.cloned.1.call-start = ((), (), s32[]{:S(2)}) async-start(), calls=%async_computation | async-start | bytes 2097152 | tf_op jit(solution)/shard_map/psum | solution.py:184
  8.2 20.2 %collective-permute-start = (bf16[45,3,128]{2,1,0:T(4,128)(2,1)S(1)}, bf16[45,3,128]{2,1,0:T(4,128)(2,1)S(1)}, u32[]{:S(2)}, u32[]{:S(2)}) collective-permute-start(bf16[45,3,128]{2,1,0:T(4,128)(2,1)S(1)} %get-tuple-element.207), channel_id=1, source_target_pairs={{0,8},{8,16},{16,24},{24,32},{32,40},{40,48},{48,56},{56,64},{64,7... | collective-permute-start | bytes 103688 | tf_op jit(solution)/shard_map/ppermute | solution.py:21
  8.3 20.1 %collective-permute-start.1 = (bf16[45,3,128]{2,1,0:T(4,128)(2,1)S(1)}, bf16[45,3,128]{2,1,0:T(4,128)(2,1)S(1)}, u32[]{:S(2)}, u32[]{:S(2)}) collective-permute-start(bf16[45,3,128]{2,1,0:T(4,128)(2,1)S(1)} %get-tuple-element.208), channel_id=1, source_target_pairs={{8,0},{16,8},{24,16},{32,24},{40,32},{48,40},{56,48},{64,56},{72,6... | collective-permute-start | bytes 103688 | tf_op jit(solution)/shard_map/ppermute | solution.py:22
  17.2 26.3 %copy-start.25 = (f32[128]{0:T(128)}, f32[128]{0:T(128)S(1)}, u32[]{:S(2)}) copy-start(f32[128]{0:T(128)S(1)} %get-tuple-element.298) | copy-start | bytes 1540
  17.2 26.3 %copy-start.27 = (f32[128]{0:T(128)}, f32[128]{0:T(128)S(1)}, u32[]{:S(2)}) copy-start(f32[128]{0:T(128)S(1)} %get-tuple-element.299) | copy-start | bytes 1540
  17.3 26.3 %copy-start.29 = (f32[128]{0:T(128)}, f32[128]{0:T(128)S(1)}, u32[]{:S(2)}) copy-start(f32[128]{0:T(128)S(1)} %get-tuple-element.300) | copy-start | bytes 1540
  17.3 26.3 %copy-start.31 = (f32[128]{0:T(128)}, f32[128]{0:T(128)S(1)}, u32[]{:S(2)}) copy-start(f32[128]{0:T(128)S(1)} %get-tuple-element.301) | copy-start | bytes 1540
  17.3 26.3 %copy-start.33 = (f32[128]{0:T(128)}, f32[128]{0:T(128)S(1)}, u32[]{:S(2)}) copy-start(f32[128]{0:T(128)S(1)} %get-tuple-element.302) | copy-start | bytes 1540
  17.3 26.3 %copy-start.35 = (f32[128]{0:T(128)}, f32[128]{0:T(128)S(1)}, u32[]{:S(2)}) copy-start(f32[128]{0:T(128)S(1)} %get-tuple-element.303) | copy-start | bytes 1540
  17.3 26.3 %copy-start.37 = (f32[128]{0:T(128)}, f32[128]{0:T(128)S(1)}, u32[]{:S(2)}) copy-start(f32[128]{0:T(128)S(1)} %get-tuple-element.304) | copy-start | bytes 1540
  17.3 26.3 %copy-start.39 = (f32[128]{0:T(128)}, f32[128]{0:T(128)S(1)}, u32[]{:S(2)}) copy-start(f32[128]{0:T(128)S(1)} %get-tuple-element.305) | copy-start | bytes 1540
  17.3 26.3 %copy-start.41 = (f32[128]{0:T(128)}, f32[128]{0:T(128)S(1)}, u32[]{:S(2)}) copy-start(f32[128]{0:T(128)S(1)} %get-tuple-element.306) | copy-start | bytes 1540
  17.3 26.3 %copy-start.43 = (f32[128]{0:T(128)}, f32[128]{0:T(128)S(1)}, u32[]{:S(2)}) copy-start(f32[128]{0:T(128)S(1)} %get-tuple-element.307) | copy-start | bytes 1540
  17.3 26.3 %copy-start.45 = (f32[128]{0:T(128)}, f32[128]{0:T(128)S(1)}, u32[]{:S(2)}) copy-start(f32[128]{0:T(128)S(1)} %get-tuple-element.308) | copy-start | bytes 1540
  17.4 26.3 %copy-start.47 = (f32[128]{0:T(128)}, f32[128]{0:T(128)S(1)}, u32[]{:S(2)}) copy-start(f32[128]{0:T(128)S(1)} %get-tuple-element.279) | copy-start | bytes 1540
  29.2 5.9 %collective-permute-start.2 = (bf16[3,30,128]{2,1,0:T(8,128)(2,1)S(1)}, bf16[3,30,128]{2,1,0:T(8,128)(2,1)S(1)}, u32[]{:S(2)}, u32[]{:S(2)}) collective-permute-start(bf16[3,30,128]{2,1,0:T(8,128)(2,1)S(1)} %get-tuple-element.198), channel_id=1, source_target_pairs={{0,1},{1,2},{2,3},{3,4},{4,5},{5,6},{6,7},{8,9},{9,10},{10,11},{11... | collective-permute-start | bytes 69128 | tf_op jit(solution)/shard_map/ppermute | solution.py:21
  32.6 5.7 %collective-permute-start.3 = (bf16[3,30,128]{2,1,0:T(8,128)(2,1)S(1)}, bf16[3,30,128]{2,1,0:T(8,128)(2,1)S(1)}, u32[]{:S(2)}, u32[]{:S(2)}) collective-permute-start(bf16[3,30,128]{2,1,0:T(8,128)(2,1)S(1)} %get-tuple-element.199), channel_id=1, source_target_pairs={{1,0},{2,1},{3,2},{4,3},{5,4},{6,5},{7,6},{9,8},{10,9},{11,10},{12... | collective-permute-start | bytes 69128 | tf_op jit(solution)/shard_map/ppermute | solution.py:22
  53.1 7.2 %collective-permute-start.4 = (bf16[45,3,128]{2,1,0:T(4,128)(2,1)S(1)}, bf16[45,3,128]{2,1,0:T(4,128)(2,1)S(1)}, u32[]{:S(2)}, u32[]{:S(2)}) collective-permute-start(bf16[45,3,128]{2,1,0:T(4,128)(2,1)S(1)} %get-tuple-element.205), channel_id=1, source_target_pairs={{0,8},{8,16},{16,24},{24,32},{32,40},{40,48},{48,56},{56,64},{64,7... | collective-permute-start | bytes 103688 | tf_op jit(solution)/shard_map/ppermute | solution.py:21
  53.2 7.1 %collective-permute-start.5 = (bf16[45,3,128]{2,1,0:T(4,128)(2,1)S(1)}, bf16[45,3,128]{2,1,0:T(4,128)(2,1)S(1)}, u32[]{:S(2)}, u32[]{:S(2)}) collective-permute-start(bf16[45,3,128]{2,1,0:T(4,128)(2,1)S(1)} %get-tuple-element.206), channel_id=1, source_target_pairs={{8,0},{16,8},{24,16},{32,24},{40,32},{48,40},{56,48},{64,56},{72,6... | collective-permute-start | bytes 103688 | tf_op jit(solution)/shard_map/ppermute | solution.py:22
  60.3 6.5 %collective-permute-start.6 = (bf16[3,30,128]{2,1,0:T(8,128)(2,1)S(1)}, bf16[3,30,128]{2,1,0:T(8,128)(2,1)S(1)}, u32[]{:S(2)}, u32[]{:S(2)}) collective-permute-start(bf16[3,30,128]{2,1,0:T(8,128)(2,1)S(1)} %get-tuple-element.194), channel_id=1, source_target_pairs={{0,1},{1,2},{2,3},{3,4},{4,5},{5,6},{6,7},{8,9},{9,10},{10,11},{11... | collective-permute-start | bytes 69128 | tf_op jit(solution)/shard_map/ppermute | solution.py:21
  63.4 6.4 %collective-permute-start.7 = (bf16[3,30,128]{2,1,0:T(8,128)(2,1)S(1)}, bf16[3,30,128]{2,1,0:T(8,128)(2,1)S(1)}, u32[]{:S(2)}, u32[]{:S(2)}) collective-permute-start(bf16[3,30,128]{2,1,0:T(8,128)(2,1)S(1)} %get-tuple-element.195), channel_id=1, source_target_pairs={{1,0},{2,1},{3,2},{4,3},{5,4},{6,5},{7,6},{9,8},{10,9},{11,10},{12... | collective-permute-start | bytes 69128 | tf_op jit(solution)/shard_map/ppermute | solution.py:22
  93.0 7.3 %collective-permute-start.8 = (bf16[45,3,128]{2,1,0:T(4,128)(2,1)S(1)}, bf16[45,3,128]{2,1,0:T(4,128)(2,1)S(1)}, u32[]{:S(2)}, u32[]{:S(2)}) collective-permute-start(bf16[45,3,128]{2,1,0:T(4,128)(2,1)S(1)} %get-tuple-element.203), channel_id=1, source_target_pairs={{0,8},{8,16},{16,24},{24,32},{32,40},{40,48},{48,56},{56,64},{64,7... | collective-permute-start | bytes 103688 | tf_op jit(solution)/shard_map/ppermute | solution.py:21
  93.1 7.3 %collective-permute-start.9 = (bf16[45,3,128]{2,1,0:T(4,128)(2,1)S(1)}, bf16[45,3,128]{2,1,0:T(4,128)(2,1)S(1)}, u32[]{:S(2)}, u32[]{:S(2)}) collective-permute-start(bf16[45,3,128]{2,1,0:T(4,128)(2,1)S(1)} %get-tuple-element.204), channel_id=1, source_target_pairs={{8,0},{16,8},{24,16},{32,24},{40,32},{48,40},{56,48},{64,56},{72,6... | collective-permute-start | bytes 103688 | tf_op jit(solution)/shard_map/ppermute | solution.py:22
  100.4 20.3 %collective-permute-start.10 = (bf16[3,30,128]{2,1,0:T(8,128)(2,1)S(1)}, bf16[3,30,128]{2,1,0:T(8,128)(2,1)S(1)}, u32[]{:S(2)}, u32[]{:S(2)}) collective-permute-start(bf16[3,30,128]{2,1,0:T(8,128)(2,1)S(1)} %get-tuple-element.190), channel_id=1, source_target_pairs={{1,0},{2,1},{3,2},{4,3},{5,4},{6,5},{7,6},{9,8},{10,9},{11,10},{12... | collective-permute-start | bytes 69128 | tf_op jit(solution)/shard_map/ppermute | solution.py:22
  102.6 18.2 %collective-permute-start.11 = (bf16[3,30,128]{2,1,0:T(8,128)(2,1)S(1)}, bf16[3,30,128]{2,1,0:T(8,128)(2,1)S(1)}, u32[]{:S(2)}, u32[]{:S(2)}) collective-permute-start(bf16[3,30,128]{2,1,0:T(8,128)(2,1)S(1)} %get-tuple-element.191), channel_id=1, source_target_pairs={{0,1},{1,2},{2,3},{3,4},{4,5},{5,6},{6,7},{8,9},{9,10},{10,11},{11... | collective-permute-start | bytes 69128 | tf_op jit(solution)/shard_map/ppermute | solution.py:21
  140.7 87.8 %copy-start.18 = (bf16[45,3,128]{2,1,0:T(4,128)(2,1)S(1)}, bf16[45,3,128]{2,1,0:T(4,128)(2,1)}, u32[]{:S(2)}) copy-start(bf16[45,3,128]{2,1,0:T(4,128)(2,1)} %get-tuple-element.201) | copy-start | bytes 103684
  140.8 101.8 %copy-start.6 = (f32[1,128,512]{2,1,0:T(8,128)S(1)}, f32[1,128,512]{2,1,0:T(8,128)}, u32[]{:S(2)}) copy-start(f32[1,128,512]{2,1,0:T(8,128)} %convolution_bitcast_fusion.3) | copy-start | bytes 786436
  228.6 2.1 collective-permute-start.13
  229.3 7.4 %collective-permute-start.12 = (bf16[45,3,128]{2,1,0:T(4,128)(2,1)S(1)}, bf16[45,3,128]{2,1,0:T(4,128)(2,1)S(1)}, u32[]{:S(2)}, u32[]{:S(2)}) collective-permute-start(bf16[45,3,128]{2,1,0:T(4,128)(2,1)S(1)} %get-tuple-element.202), channel_id=1, source_target_pairs={{0,8},{8,16},{16,24},{24,32},{32,40},{40,48},{48,56},{56,64},{64,7... | collective-permute-start | bytes 103688 | tf_op jit(solution)/shard_map/ppermute | solution.py:21
  236.7 7.4 %collective-permute-start.14 = (bf16[3,30,128]{2,1,0:T(8,128)(2,1)S(1)}, bf16[3,30,128]{2,1,0:T(8,128)(2,1)S(1)}, u32[]{:S(2)}, u32[]{:S(2)}) collective-permute-start(bf16[3,30,128]{2,1,0:T(8,128)(2,1)S(1)} %get-tuple-element.186), channel_id=1, source_target_pairs={{1,0},{2,1},{3,2},{4,3},{5,4},{6,5},{7,6},{9,8},{10,9},{11,10},{12... | collective-permute-start | bytes 69128 | tf_op jit(solution)/shard_map/ppermute | solution.py:22
  239.3 5.7 %collective-permute-start.15 = (bf16[3,30,128]{2,1,0:T(8,128)(2,1)S(1)}, bf16[3,30,128]{2,1,0:T(8,128)(2,1)S(1)}, u32[]{:S(2)}, u32[]{:S(2)}) collective-permute-start(bf16[3,30,128]{2,1,0:T(8,128)(2,1)S(1)} %get-tuple-element.187), channel_id=1, source_target_pairs={{0,1},{1,2},{2,3},{3,4},{4,5},{5,6},{6,7},{8,9},{9,10},{10,11},{11... | collective-permute-start | bytes 69128 | tf_op jit(solution)/shard_map/ppermute | solution.py:21
  (171 other events, 2235.0 us)
Sparse Core Ops, SparseCore 0:
  244.2 254.5 all-reduce.3
where the time goes:
time: 517 us; the launch traced here: 510 us
  waiting for transfers between devices  262 us (51%)
  blocking collectives  81.3 us (16%)
  starting transfers between devices  52.5 us (10%)
  other arithmetic  52.3 us (10%)
  matrix products  25.1 us (5%)
  local copies, waits for them, and re-layouts  18.7 us (4%)
  between operations  17.3 us (3%)
    psum x1, waiting for transfers between devices, sum_everything(): lax.psum((kernel_part, conv_part, gain_part, shift_part, first_part, firs...  247 us
    psum x1, blocking collectives, sum_everything(): lax.psum((kernel_part, conv_part, gain_part, shift_part, first_part, firs...  81.3 us
    ppermute x8, starting transfers between devices, with_halo(): after = lax.ppermute(first, axis, down)  29.4 us
    ppermute x8, starting transfers between devices, with_halo(): before = lax.ppermute(last, axis, up)  23 us
    dot_general x2, matrix products, block_forward(): jnp.dot(lifted, weight_in, preferred_element_type=jnp.float32) + bias_in  13 us
  transfers between devices with their start and end apart: 17, of which 7 were waited for; matrix products, arithmetic and copies ran while one was open for 5% of the time, Pallas kernels for 0%

commit v1 on v0

--- a/solution.py
+++ b/solution.py
@@ -182,18 +182,21 @@
         scale_part,
     ) = parts
     return lax.psum(
-        (
-            kernel_part,
-            conv_part,
-            gain_part,
-            shift_part,
-            first_part,
-            first_bias,
-            second_part,
-            second_bias,
-            scale_part,
+        lax.psum(
+            (
+                kernel_part,
+                conv_part,
+                gain_part,
+                shift_part,
+                first_part,
+                first_bias,
+                second_part,
+                second_bias,
+                scale_part,
+            ),
+            "lon",
         ),
-        ("lon", "lat"),
+        "lat",
     )
 
 

time: 517 us -> 690 us (1.33)
  waiting for transfers between devices: 262 us -> 348 us
  blocking collectives: 81.3 us -> 166 us
    psum x0 -> x1, waiting for transfers between devices: none -> 76.3 us  [sum_everything(): lax.psum(lax.psum((kernel_part, conv_part, gain_part, shift_part, first_p...]
    psum x1, blocking collectives: 81.3 us -> 133 us  [sum_everything(): lax.psum((kernel_part, conv_part, gain_part, shift_part, first_part, firs...]
    psum x0 -> x1, blocking collectives: none -> 33 us  [sum_everything(): lax.psum(lax.psum((kernel_part, conv_part, gain_part, shift_part, first_p...]
    psum x1, waiting for transfers between devices: 247 us -> 260 us  [sum_everything(): lax.psum((kernel_part, conv_part, gain_part, shift_part, first_part, firs...]
  transfers between devices with their start and end apart: 17 -> 18, of which waited for: 7 -> 7; matrix products, arithmetic and copies ran while one was open for 5% -> 4% of each run, Pallas kernels for 0% -> 0%
where the time goes in v1:
time: 690 us; the launch traced here: 681 us
  waiting for transfers between devices  348 us (50%)
  blocking collectives  166 us (24%)
  starting transfers between devices  54.6 us (8%)
  other arithmetic  52.3 us (8%)
  matrix products  24.7 us (4%)
  local copies, waits for them, and re-layouts  18 us (3%)
  between operations  17.4 us (3%)
    psum x1, waiting for transfers between devices, sum_everything(): lax.psum((kernel_part, conv_part, gain_part, shift_part, first_part, firs...  260 us
    psum x1, blocking collectives, sum_everything(): lax.psum((kernel_part, conv_part, gain_part, shift_part, first_part, firs...  133 us
    psum x1, waiting for transfers between devices, sum_everything(): lax.psum(lax.psum((kernel_part, conv_part, gain_part, shift_part, first_p...  76.3 us
    psum x1, blocking collectives, sum_everything(): lax.psum(lax.psum((kernel_part, conv_part, gain_part, shift_part, first_p...  33 us
    ppermute x8, starting transfers between devices, with_halo(): after = lax.ppermute(first, axis, down)  30.6 us
    ppermute x8, starting transfers between devices, with_halo(): before = lax.ppermute(last, axis, up)  23.9 us
  transfers between devices with their start and end apart: 18, of which 7 were waited for; matrix products, arithmetic and copies ran while one was open for 4% of the time, Pallas kernels for 0%

profile of v1, /device:TPU:2, one launch (start us, length us, event | category | flops | bytes accessed | tf_op | source)
XLA Modules:
  0.0 681.0 jit_solution(319241393124355971)
XLA Ops:
  8.3 8.0 %collective-permute-start.1 = (bf16[45,3,128]{2,1,0:T(4,128)(2,1)S(1)}, bf16[45,3,128]{2,1,0:T(4,128)(2,1)S(1)}, u32[]{:S(2)}, u32[]{:S(2)}) collective-permute-start(bf16[45,3,128]{2,1,0:T(4,128)(2,1)S(1)} %get-tuple-element.217), channel_id=1, source_target_pairs={{8,0},{16,8},{24,16},{32,24},{40,32},{48,40},{56,48},{64,56},{72,6... | collective-permute-start | bytes 103688 | tf_op jit(solution)/shard_map/ppermute | solution.py:22
  24.9 2.5 convert_reduce_fusion.3
  29.2 3.4 collective-permute-start.2
  32.6 2.4 collective-permute-start.3
  35.1 3.2 collective-permute-done.3
  38.6 5.0 fusion.421
  44.7 6.0 fusion.4
  53.2 5.3 collective-permute-start.5
  60.3 3.1 collective-permute-start.6
  63.4 3.1 collective-permute-start.7
  66.8 3.1 collective-permute-done.7
  70.1 5.0 fusion.419
  78.7 7.0 %fusion.7 = (bf16[1080,512]{1,0:T(8,128)(2,1)}, f32[1080,512]{1,0:T(8,128)S(1)}) fusion(f32[512]{0:T(512)} %bitcast.780, bf16[1080,128]{1,0:T(8,128)(2,1)S(1)} %bitcast.741, bf16[2,128,512]{2,1,0:T(8,128)(2,1)} %param.19), kind=kOutput, calls=%fused_computation.116 | convolution fusion | flops 178053120 | bytes 3727360 | tf_op jit(solution)/shard_map/dot_general | solution.py:60
  85.7 1.9 convert_reduce_fusion
  93.1 5.3 collective-permute-start.9
  98.5 1.7 fusion.200
  100.4 2.2 collective-permute-start.10
  102.6 12.7 %collective-permute-start.11 = (bf16[3,30,128]{2,1,0:T(8,128)(2,1)S(1)}, bf16[3,30,128]{2,1,0:T(8,128)(2,1)S(1)}, u32[]{:S(2)}, u32[]{:S(2)}) collective-permute-start(bf16[3,30,128]{2,1,0:T(8,128)(2,1)S(1)} %get-tuple-element.200), channel_id=1, source_target_pairs={{0,1},{1,2},{2,3},{3,4},{4,5},{5,6},{6,7},{8,9},{9,10},{10,11},{11... | collective-permute-start | bytes 69128 | tf_op jit(solution)/shard_map/ppermute | solution.py:21
  115.8 4.9 stack.474
  122.0 6.2 multiply_convert_fusion.1
  128.5 1.9 convert_reduce_fusion.1
  137.0 2.4 multiply_reduce_fusion.1
  142.7 133.3 %all-reduce = (f32[2,7,7,128]{3,2,1,0:T(8,128)S(1)}, f32[2,128]{1,0:T(2,128)S(1)}, f32[2,128]{1,0:T(2,128)S(1)}, f32[2,128]{1,0:T(2,128)S(1)}, f32[2,512]{1,0:T(...) all-reduce(f32[2,7,7,128]{3,2,1,0:T(8,128)S(1)} %pad_maximum_fusion, ...), channel_id=1, replica_groups=mesh['lon'=32,'lat'=8] {'lon'}, use_global_device_ids=true, to_apply=%region_106.0 | all-reduce | flops 14848 | bytes 118784 | tf_op jit(solution)/shard_map/psum | solution.py:185
  276.0 33.0 %all-reduce.2 = (f32[2,7,7,128]{3,2,1,0:T(8,128)S(1)}, f32[2,128]{1,0:T(2,128)S(1)}, f32[2,128]{1,0:T(2,128)S(1)}, f32[2,128]{1,0:T(2,128)S(1)}, f32[2,512]{1,0:...) all-reduce(f32[2,7,7,128]{3,2,1,0:T(8,128)S(1)} %get-tuple-element., ...), channel_id=1, replica_groups=mesh['lon'=32,'lat'=8] {'lat'}, use_global_device_ids=true, to_apply=%region_107.0 | all-reduce | flops 14848 | bytes 118784 | tf_op jit(solution)/shard_map/psum | solution.py:184
  314.4 3.4 collective-permute-done.12
  317.9 4.2 collective-permute-start.14
  322.1 3.9 collective-permute-start.15
  328.0 259.8 %all-reduce.7.cloned.1.call-done = (f32[2,128,512]{2,1,0:T(8,128)}, f32[2,512,128]{2,1,0:T(8,128)}) async-done(((f32[2,128,512]{2,1,0:T(8,128)}, f32[2,512,128]{2,1,0:T(8,128)}), (f32[2,128,512]{2,1,0:T(8,128)}, f32[2,512,128]{2,1,0:T(8,128)})) %all-reduce.7.cloned.1.call-update) | async-done | bytes 1048592 | tf_op jit(solution)/shard_map/psum | solution.py:185
  588.1 5.8 fusion.280
  593.9 76.3 %all-reduce.9.cloned.1.call-done = (f32[2,128,512]{2,1,0:T(8,128)}, f32[2,512,128]{2,1,0:T(8,128)}) async-done(((f32[2,128,512]{2,1,0:T(8,128)}, f32[2,512,128]{2,1,0:T(8,128)}), (f32[2,128,512]{2,1,0:T(8,128)}, f32[2,512,128]{2,1,0:T(8,128)})) %all-reduce.9.cloned.1.call-update) | async-done | bytes 1048592 | tf_op jit(solution)/shard_map/psum | solution.py:184
  670.2 1.9 broadcast_multiply_fusion.1
  672.1 1.9 broadcast_multiply_fusion
  (472 shorter events, 43.9 us)
Async XLA Ops:
  7.2 580.6 %all-reduce.7.cloned.1.call-start = ((), (), s32[]{:S(2)}) async-start(), calls=%async_computation | async-start | bytes 2097152 | tf_op jit(solution)/shard_map/psum | solution.py:185
  8.2 20.2 %collective-permute-start = (bf16[45,3,128]{2,1,0:T(4,128)(2,1)S(1)}, bf16[45,3,128]{2,1,0:T(4,128)(2,1)S(1)}, u32[]{:S(2)}, u32[]{:S(2)}) collective-permute-start(bf16[45,3,128]{2,1,0:T(4,128)(2,1)S(1)} %get-tuple-element.216), channel_id=1, source_target_pairs={{0,8},{8,16},{16,24},{24,32},{32,40},{40,48},{48,56},{56,64},{64,7... | collective-permute-start | bytes 103688 | tf_op jit(solution)/shard_map/ppermute | solution.py:21
  8.3 20.1 %collective-permute-start.1 = (bf16[45,3,128]{2,1,0:T(4,128)(2,1)S(1)}, bf16[45,3,128]{2,1,0:T(4,128)(2,1)S(1)}, u32[]{:S(2)}, u32[]{:S(2)}) collective-permute-start(bf16[45,3,128]{2,1,0:T(4,128)(2,1)S(1)} %get-tuple-element.217), channel_id=1, source_target_pairs={{8,0},{16,8},{24,16},{32,24},{40,32},{48,40},{56,48},{64,56},{72,6... | collective-permute-start | bytes 103688 | tf_op jit(solution)/shard_map/ppermute | solution.py:22
  29.2 5.9 collective-permute-start.2
  32.6 5.7 collective-permute-start.3
  53.1 7.2 %collective-permute-start.4 = (bf16[45,3,128]{2,1,0:T(4,128)(2,1)S(1)}, bf16[45,3,128]{2,1,0:T(4,128)(2,1)S(1)}, u32[]{:S(2)}, u32[]{:S(2)}) collective-permute-start(bf16[45,3,128]{2,1,0:T(4,128)(2,1)S(1)} %get-tuple-element.214), channel_id=1, source_target_pairs={{0,8},{8,16},{16,24},{24,32},{32,40},{40,48},{48,56},{56,64},{64,7... | collective-permute-start | bytes 103688 | tf_op jit(solution)/shard_map/ppermute | solution.py:21
  53.2 7.1 %collective-permute-start.5 = (bf16[45,3,128]{2,1,0:T(4,128)(2,1)S(1)}, bf16[45,3,128]{2,1,0:T(4,128)(2,1)S(1)}, u32[]{:S(2)}, u32[]{:S(2)}) collective-permute-start(bf16[45,3,128]{2,1,0:T(4,128)(2,1)S(1)} %get-tuple-element.215), channel_id=1, source_target_pairs={{8,0},{16,8},{24,16},{32,24},{40,32},{48,40},{56,48},{64,56},{72,6... | collective-permute-start | bytes 103688 | tf_op jit(solution)/shard_map/ppermute | solution.py:22
  60.3 6.5 collective-permute-start.6
  63.4 6.4 collective-permute-start.7
  93.0 7.3 %collective-permute-start.8 = (bf16[45,3,128]{2,1,0:T(4,128)(2,1)S(1)}, bf16[45,3,128]{2,1,0:T(4,128)(2,1)S(1)}, u32[]{:S(2)}, u32[]{:S(2)}) collective-permute-start(bf16[45,3,128]{2,1,0:T(4,128)(2,1)S(1)} %get-tuple-element.212), channel_id=1, source_target_pairs={{0,8},{8,16},{16,24},{24,32},{32,40},{40,48},{48,56},{56,64},{64,7... | collective-permute-start | bytes 103688 | tf_op jit(solution)/shard_map/ppermute | solution.py:21
  93.1 7.2 %collective-permute-start.9 = (bf16[45,3,128]{2,1,0:T(4,128)(2,1)S(1)}, bf16[45,3,128]{2,1,0:T(4,128)(2,1)S(1)}, u32[]{:S(2)}, u32[]{:S(2)}) collective-permute-start(bf16[45,3,128]{2,1,0:T(4,128)(2,1)S(1)} %get-tuple-element.213), channel_id=1, source_target_pairs={{8,0},{16,8},{24,16},{32,24},{40,32},{48,40},{56,48},{64,56},{72,6... | collective-permute-start | bytes 103688 | tf_op jit(solution)/shard_map/ppermute | solution.py:22
  100.4 20.3 %collective-permute-start.10 = (bf16[3,30,128]{2,1,0:T(8,128)(2,1)S(1)}, bf16[3,30,128]{2,1,0:T(8,128)(2,1)S(1)}, u32[]{:S(2)}, u32[]{:S(2)}) collective-permute-start(bf16[3,30,128]{2,1,0:T(8,128)(2,1)S(1)} %get-tuple-element.199), channel_id=1, source_target_pairs={{1,0},{2,1},{3,2},{4,3},{5,4},{6,5},{7,6},{9,8},{10,9},{11,10},{12... | collective-permute-start | bytes 69128 | tf_op jit(solution)/shard_map/ppermute | solution.py:22
  102.6 18.2 %collective-permute-start.11 = (bf16[3,30,128]{2,1,0:T(8,128)(2,1)S(1)}, bf16[3,30,128]{2,1,0:T(8,128)(2,1)S(1)}, u32[]{:S(2)}, u32[]{:S(2)}) collective-permute-start(bf16[3,30,128]{2,1,0:T(8,128)(2,1)S(1)} %get-tuple-element.200), channel_id=1, source_target_pairs={{0,1},{1,2},{2,3},{3,4},{4,5},{5,6},{6,7},{8,9},{9,10},{10,11},{11... | collective-permute-start | bytes 69128 | tf_op jit(solution)/shard_map/ppermute | solution.py:21
  310.7 3.7 collective-permute-start.13
  310.7 7.1 %collective-permute-start.12 = (bf16[45,3,128]{2,1,0:T(4,128)(2,1)S(1)}, bf16[45,3,128]{2,1,0:T(4,128)(2,1)S(1)}, u32[]{:S(2)}, u32[]{:S(2)}) collective-permute-start(bf16[45,3,128]{2,1,0:T(4,128)(2,1)S(1)} %get-tuple-element.211), channel_id=1, source_target_pairs={{0,8},{8,16},{16,24},{24,32},{32,40},{40,48},{48,56},{56,64},{64,7... | collective-permute-start | bytes 103688 | tf_op jit(solution)/shard_map/ppermute | solution.py:21
  312.9 274.9 %copy-start.33 = (f32[128]{0:T(128)S(1)}, f32[128]{0:T(128)}, u32[]{:S(2)}) copy-start(f32[128]{0:T(128)} %copy-done.32) | copy-start | bytes 1540
  312.9 274.9 %copy-start.35 = (f32[128]{0:T(128)S(1)}, f32[128]{0:T(128)}, u32[]{:S(2)}) copy-start(f32[128]{0:T(128)} %copy-done.34) | copy-start | bytes 1540
  312.9 274.9 %copy-start.37 = (f32[128]{0:T(128)S(1)}, f32[128]{0:T(128)}, u32[]{:S(2)}) copy-start(f32[128]{0:T(128)} %copy-done.36) | copy-start | bytes 1540
  312.9 274.9 %copy-start.39 = (f32[128]{0:T(128)S(1)}, f32[128]{0:T(128)}, u32[]{:S(2)}) copy-start(f32[128]{0:T(128)} %copy-done.38) | copy-start | bytes 1540
  312.9 274.9 %copy-start.41 = (f32[128]{0:T(128)S(1)}, f32[128]{0:T(128)}, u32[]{:S(2)}) copy-start(f32[128]{0:T(128)} %copy-done.40) | copy-start | bytes 1540
  313.0 274.9 %copy-start.43 = (f32[128]{0:T(128)S(1)}, f32[128]{0:T(128)}, u32[]{:S(2)}) copy-start(f32[128]{0:T(128)} %copy-done.42) | copy-start | bytes 1540
  313.0 274.9 %copy-start.45 = (f32[128]{0:T(128)S(1)}, f32[128]{0:T(128)}, u32[]{:S(2)}) copy-start(f32[128]{0:T(128)} %copy-done.44) | copy-start | bytes 1540
  313.0 274.9 %copy-start.47 = (f32[128]{0:T(128)S(1)}, f32[128]{0:T(128)}, u32[]{:S(2)}) copy-start(f32[128]{0:T(128)} %copy-done.46) | copy-start | bytes 1540
  313.0 274.9 %copy-start.49 = (f32[128]{0:T(128)S(1)}, f32[128]{0:T(128)}, u32[]{:S(2)}) copy-start(f32[128]{0:T(128)} %copy-done.48) | copy-start | bytes 1540
  313.0 274.9 %copy-start.51 = (f32[128]{0:T(128)S(1)}, f32[128]{0:T(128)}, u32[]{:S(2)}) copy-start(f32[128]{0:T(128)} %copy-done.50) | copy-start | bytes 1540
  313.0 274.9 %copy-start.53 = (f32[128]{0:T(128)S(1)}, f32[128]{0:T(128)}, u32[]{:S(2)}) copy-start(f32[128]{0:T(128)} %copy-done.52) | copy-start | bytes 1540
  313.0 274.9 %copy-start.55 = (f32[128]{0:T(128)S(1)}, f32[128]{0:T(128)}, u32[]{:S(2)}) copy-start(f32[128]{0:T(128)} %copy-done.54) | copy-start | bytes 1540
  313.0 274.9 %copy-start.57 = (f32[128]{0:T(128)S(1)}, f32[128]{0:T(128)}, u32[]{:S(2)}) copy-start(f32[128]{0:T(128)} %copy-done.56) | copy-start | bytes 1540
  313.0 274.9 %copy-start.59 = (f32[128]{0:T(128)S(1)}, f32[128]{0:T(128)}, u32[]{:S(2)}) copy-start(f32[128]{0:T(128)} %copy-done.58) | copy-start | bytes 1540
  313.3 356.9 %all-reduce.9.cloned.1.call-start = ((), (), s32[]{:S(2)}) async-start(), calls=%async_computation.1 | async-start | bytes 2097152 | tf_op jit(solution)/shard_map/psum | solution.py:184
  317.9 9.4 %collective-permute-start.14 = (bf16[3,30,128]{2,1,0:T(8,128)(2,1)S(1)}, bf16[3,30,128]{2,1,0:T(8,128)(2,1)S(1)}, u32[]{:S(2)}, u32[]{:S(2)}) collective-permute-start(bf16[3,30,128]{2,1,0:T(8,128)(2,1)S(1)} %get-tuple-element.195), channel_id=1, source_target_pairs={{1,0},{2,1},{3,2},{4,3},{5,4},{6,5},{7,6},{9,8},{10,9},{11,10},{12... | collective-permute-start | bytes 69128 | tf_op jit(solution)/shard_map/ppermute | solution.py:22
  322.1 5.7 collective-permute-start.15
  (172 other events, 8468.5 us)
Sparse Core Ops, SparseCore 0:
  313.4 274.3 all-reduce.6
  590.6 79.5 all-reduce.8
